TPU v7x, 32 devices: a whole 2x2x4 slice. The times are simulated.
32 devices in a mesh: dp: 8 (over z, x), tensor: 4 (over y, core).
Axes of the slice: x: 2, y: 2, z: 4, core: 2. Of those that a mesh axis runs over, the one named last changes fastest.
Arguments:
- tokens: bfloat16 [16, 1024, 2048], P('dp', 'tensor'), may hold values from -6 to 6
- pre_gain: float32 [2048], replicated, may hold values from 0.1 to 1.9
- weight_gate: bfloat16 [2048, 4096], P(None, 'tensor'), may hold values from -0.125 to 0.125
- weight_inner: bfloat16 [2048, 4096], P(None, 'tensor'), may hold values from -0.125 to 0.125
- weight_step: bfloat16 [2048, 64], P(None, 'tensor'), may hold values from -0.0625 to 0.0625
- weight_shared: bfloat16 [2048, 256], replicated, may hold values from -0.125 to 0.125
- conv_kernel: float32 [4, 4096], P(None, 'tensor'), may hold values from -3 to 3
- conv_offset: float32 [4096], P('tensor'), may hold values from -1.8 to 1.8
- shared_kernel: float32 [4, 256], replicated, may hold values from -3 to 3
- shared_offset: float32 [256], replicated, may hold values from -1.8 to 1.8
- step_bias: float32 [64], P('tensor'), may hold values from -7 to -2.3
- log_rate: float32 [64], P('tensor'), may hold values from 0 to 2.77
- skip_gain: float32 [64], P('tensor'), may hold values from 0.5 to 2
- gate_gain: float32 [4096], P('tensor'), may hold values from 0.1 to 1.9
- weight_out: bfloat16 [4096, 2048], P('tensor'), may hold values from -0.09375 to 0.09375
- cotangent: bfloat16 [16, 1024, 2048], P('dp', 'tensor'), may hold values from -6 to 6
- segments: int32 [16, 1024], P('dp'), may hold values from 0 to 7, never falling along the last dimension, each value on 1 to 512 neighbouring positions
- image_span: int32 [16, 2], P('dp'), may hold values from 0 to 4, as said below
Outputs:
- block_out: bfloat16 [16, 1024, 2048], P('dp', 'tensor')
- tokens_grad: bfloat16 [16, 1024, 2048], P('dp', 'tensor')
- pre_gain_grad: float32 [2048], replicated
- weight_gate_grad: float32 [2048, 4096], P(None, 'tensor')
- weight_inner_grad: float32 [2048, 4096], P(None, 'tensor')
- weight_step_grad: float32 [2048, 64], P(None, 'tensor')
- weight_shared_grad: float32 [2048, 256], replicated
- conv_kernel_grad: float32 [4, 4096], P(None, 'tensor')
- conv_offset_grad: float32 [4096], P('tensor')
- shared_kernel_grad: float32 [4, 256], replicated
- shared_offset_grad: float32 [256], replicated
- step_bias_grad: float32 [64], P('tensor')
- log_rate_grad: float32 [64], P('tensor')
- skip_gain_grad: float32 [64], P('tensor')
- gate_gain_grad: float32 [4096], P('tensor')
- weight_out_grad: float32 [4096, 2048], P('tensor')
Inputs may be any that keep to these rules, and one draw needn't show every extreme that they name: `segments`: along a sequence the document ids never fall; a document has 1 to 512 tokens. `image_span`: each row holds (first image piece, number of image pieces); first + number <= 4; a sequence may have no image piece.
All inputs are finite; a program needn't handle non-finite values.
Results may differ from a plain program's by a relative error of at most 0.0087.
Values may be sent and summed in bfloat16 or wider, within the bound.
No kernel may reach another device: no remote copies, remote signals or barrier semaphores. Data moves between devices by JAX's collectives and lax.ppermute only.
A program may use at most 320 MiB of HBM per device.

v0:
```python
from functools import partial
import jax
import jax.numpy as jnp
from jax import lax
from jax.sharding import PartitionSpec as P

STRETCH = 256
EPSILON = 1e-05
HIGHEST = lax.Precision.HIGHEST
CONTRACT_ROWS = (((0,), (0,)), ((), ()))
CONTRACT_COLUMNS = (((1,), (1,)), ((), ()))


def sigmoid_linear(values):
    return values * jax.nn.sigmoid(values)


def causal_conv(signal, kernel, offset):
    length = signal.shape[0]
    tap_count = kernel.shape[0]
    padded = jnp.pad(signal, ((tap_count - 1, 0), (0, 0)))
    summed = offset[None, :] + kernel[0][None, :] * padded[0:length]
    for tap_index in range(1, tap_count):
        summed = summed + kernel[tap_index][None, :] * padded[tap_index : tap_index + length]
    return summed


def piece_flags(span_row, pieces):
    piece_index = jnp.arange(pieces, dtype=jnp.int32)
    inside = (piece_index >= span_row[0]) & (piece_index < span_row[0] + span_row[1])
    return inside.astype(jnp.int32)


def state_scan(inputs_x, step_size, decay_rate, b_matrix, c_matrix, segment, is_image):
    length, head_count, head_width = inputs_x.shape
    pieces = is_image.shape[0]
    block_len = length // pieces
    log_step = (step_size * decay_rate[None, :]).reshape(pieces, block_len, head_count)
    cumulated = jnp.cumsum(jnp.transpose(log_step, (2, 0, 1)), axis=2)
    weighted_x = jnp.transpose(
        (inputs_x * step_size[:, :, None]).reshape(pieces, block_len, head_count, head_width),
        (2, 0, 1, 3),
    )
    b_blocks = b_matrix.reshape(pieces, block_len, -1)
    c_blocks = c_matrix.reshape(pieces, block_len, -1)
    doc_blocks = segment.reshape(pieces, block_len)
    same_doc = doc_blocks[:, :, None] == doc_blocks[:, None, :]
    position = jnp.arange(block_len)
    causal = position[:, None] >= position[None, :]
    allowed = same_doc & (causal[None, :, :] | (is_image[:, None, None] > 0))
    spread = cumulated[:, :, :, None] - cumulated[:, :, None, :]
    decays = jnp.where(allowed[None, :, :, :], jnp.exp(-jnp.abs(spread)), jnp.zeros_like(spread))
    scores = jnp.einsum("ctn,csn->cts", c_blocks, b_blocks, precision=HIGHEST)
    mixing = scores[None, :, :, :] * decays
    within = jnp.einsum("hcts,hcsp->hctp", mixing, weighted_x, precision=HIGHEST)
    last_doc = doc_blocks[:, -1]
    to_end = (doc_blocks == last_doc[:, None]).astype(cumulated.dtype)[None, :, :] * jnp.exp(
        cumulated[:, :, -1:] - cumulated
    )
    fresh_state = jnp.einsum(
        "hcsp,csn->chpn", to_end[:, :, :, None] * weighted_x, b_blocks, precision=HIGHEST
    )
    before_doc = jnp.concatenate([doc_blocks[:1, 0], doc_blocks[:-1, -1]])
    keep_factor = (last_doc == before_doc).astype(cumulated.dtype)[:, None] * jnp.transpose(
        jnp.exp(cumulated[:, :, -1])
    )

    def advance(carry_state, scan_item):
        factor, update = scan_item
        return (factor[:, None, None] * carry_state + update, carry_state)

    start_state = jnp.zeros((head_count, head_width, b_blocks.shape[2]), inputs_x.dtype)
    final_state, entering = lax.scan(advance, start_state, (keep_factor, fresh_state))
    reach_gate = (doc_blocks == before_doc[:, None]).astype(cumulated.dtype)[None, :, :] * jnp.exp(
        cumulated
    )
    carried = (
        jnp.einsum("ctn,chpn->hctp", c_blocks, entering, precision=HIGHEST)
        * reach_gate[:, :, :, None]
    )
    total = jnp.transpose(within + carried, (1, 2, 0, 3))
    return total.reshape(length, head_count, head_width)


def state_mixer(
    segment,
    is_image,
    gate_pre,
    inner_pre,
    step_pre,
    shared_pre,
    conv_kernel,
    conv_offset,
    shared_kernel,
    shared_offset,
    step_bias,
    log_rate,
    skip_gain,
):
    activated = sigmoid_linear(causal_conv(inner_pre, conv_kernel, conv_offset))
    shared = sigmoid_linear(causal_conv(shared_pre, shared_kernel, shared_offset))
    state_width = shared.shape[1] // 2
    head_count = step_bias.shape[0]
    length = inner_pre.shape[0]
    inputs_x = activated.reshape(length, head_count, -1)
    step_size = jax.nn.softplus(step_pre + step_bias[None, :])
    decay_rate = -jnp.exp(log_rate)
    mixed_out = state_scan(
        inputs_x,
        step_size,
        decay_rate,
        shared[:, :state_width],
        shared[:, state_width:],
        segment,
        is_image,
    )
    mixed_out = mixed_out + skip_gain[None, :, None] * inputs_x
    return mixed_out.reshape(length, -1) * sigmoid_linear(gate_pre)


def body(
    tokens,
    pre_gain,
    weight_gate,
    weight_inner,
    weight_step,
    weight_shared,
    conv_kernel,
    conv_offset,
    shared_kernel,
    shared_offset,
    step_bias,
    log_rate,
    skip_gain,
    gate_gain,
    weight_out,
    cotangent,
    segments,
    image_span,
):
    micro_count = tokens.shape[0]
    row_count = tokens.shape[1]
    model_width = tokens.shape[2]
    inner_width = weight_gate.shape[1] * lax.axis_size("tensor")
    pieces = segments.shape[1] // STRETCH
    rank_start = lax.axis_index("tensor") * row_count
    running = [
        jnp.zeros(parameter.shape, jnp.float32)
        for parameter in (
            pre_gain,
            weight_gate,
            weight_inner,
            weight_step,
            weight_shared,
            conv_kernel,
            conv_offset,
            shared_kernel,
            shared_offset,
            step_bias,
            log_rate,
            skip_gain,
            gate_gain,
            weight_out,
        )
    ]
    outputs = []
    input_grads = []
    for micro_index in range(micro_count):
        own_rows = tokens[micro_index].astype(jnp.float32)
        row_scale = lax.rsqrt(jnp.mean(own_rows * own_rows, axis=1, keepdims=True) + EPSILON)
        normed_rows = (own_rows * row_scale * pre_gain[None, :]).astype(jnp.bfloat16)
        normed_in = lax.all_gather(normed_rows, "tensor", axis=0, tiled=True)
        gate_pre = jnp.dot(normed_in, weight_gate, preferred_element_type=jnp.float32)
        inner_pre = jnp.dot(normed_in, weight_inner, preferred_element_type=jnp.float32)
        step_pre = jnp.dot(normed_in, weight_step, preferred_element_type=jnp.float32)
        shared_pre = jnp.dot(normed_in, weight_shared, preferred_element_type=jnp.float32)
        is_image = piece_flags(image_span[micro_index], pieces)
        gated_out, mixer_pullback = jax.vjp(
            partial(state_mixer, segments[micro_index], is_image),
            gate_pre,
            inner_pre,
            step_pre,
            shared_pre,
            conv_kernel,
            conv_offset,
            shared_kernel,
            shared_offset,
            step_bias,
            log_rate,
            skip_gain,
        )
        square_sum = lax.psum(jnp.sum(gated_out * gated_out, axis=1), "tensor")
        gate_scale = lax.rsqrt(square_sum / inner_width + EPSILON)[:, None]
        normed_out = (gated_out * gate_scale * gate_gain[None, :]).astype(jnp.bfloat16)
        mixed_rows = lax.psum_scatter(
            jnp.dot(normed_out, weight_out, preferred_element_type=jnp.float32),
            "tensor",
            scatter_dimension=0,
            tiled=True,
        )
        outputs.append((own_rows + mixed_rows).astype(jnp.bfloat16))
        cot_rows = cotangent[micro_index]
        cot_full = lax.all_gather(cot_rows, "tensor", axis=0, tiled=True)
        normed_grad = lax.dot_general(
            cot_full, weight_out, CONTRACT_COLUMNS, preferred_element_type=jnp.float32
        )
        running[13] = running[13] + lax.dot_general(
            normed_out, cot_full, CONTRACT_ROWS, preferred_element_type=jnp.float32
        )
        running[12] = running[12] + jnp.sum(normed_grad * gated_out * gate_scale, axis=0)
        scaled_grad = normed_grad * gate_gain[None, :]
        coupling = lax.psum(jnp.sum(scaled_grad * gated_out, axis=1), "tensor")
        cubed_scale = gate_scale * gate_scale * gate_scale
        gated_grad = (
            gate_scale * scaled_grad - cubed_scale / inner_width * gated_out * coupling[:, None]
        )
        pieces_grad = mixer_pullback(gated_grad)
        for slot_index in range(4, 11):
            running[slot_index + 1] = running[slot_index + 1] + pieces_grad[slot_index]
        shared_full = lax.psum(pieces_grad[3], "tensor")
        gate_low = pieces_grad[0].astype(jnp.bfloat16)
        inner_low = pieces_grad[1].astype(jnp.bfloat16)
        step_low = pieces_grad[2].astype(jnp.bfloat16)
        shared_low = shared_full.astype(jnp.bfloat16)
        running[1] = running[1] + lax.dot_general(
            normed_in, gate_low, CONTRACT_ROWS, preferred_element_type=jnp.float32
        )
        running[2] = running[2] + lax.dot_general(
            normed_in, inner_low, CONTRACT_ROWS, preferred_element_type=jnp.float32
        )
        running[3] = running[3] + lax.dot_general(
            normed_in, step_low, CONTRACT_ROWS, preferred_element_type=jnp.float32
        )
        running[4] = running[4] + lax.dot_general(
            normed_in, shared_low, CONTRACT_ROWS, preferred_element_type=jnp.float32
        )
        summed = lax.dot_general(
            gate_low, weight_gate, CONTRACT_COLUMNS, preferred_element_type=jnp.float32
        )
        summed = summed + lax.dot_general(
            inner_low, weight_inner, CONTRACT_COLUMNS, preferred_element_type=jnp.float32
        )
        input_part = lax.psum_scatter(
            summed
            + lax.dot_general(
                step_low, weight_step, CONTRACT_COLUMNS, preferred_element_type=jnp.float32
            ),
            "tensor",
            scatter_dimension=0,
            tiled=True,
        )
        shared_rows = lax.dynamic_slice_in_dim(shared_low, rank_start, row_count, 0)
        normed_in_grad = input_part + lax.dot_general(
            shared_rows, weight_shared, CONTRACT_COLUMNS, preferred_element_type=jnp.float32
        )
        weighted_grad = normed_in_grad * pre_gain[None, :]
        projection = jnp.sum(weighted_grad * own_rows, axis=1, keepdims=True)
        cubed_row = row_scale * row_scale * row_scale
        own_grad = row_scale * weighted_grad - cubed_row / model_width * own_rows * projection
        running[0] = running[0] + jnp.sum(normed_in_grad * own_rows * row_scale, axis=0)
        input_grads.append((cot_rows.astype(jnp.float32) + own_grad).astype(jnp.bfloat16))
    reduced = lax.psum(
        (
            running[1],
            running[2],
            running[3],
            running[4],
            running[5],
            running[6],
            running[9],
            running[10],
            running[11],
            running[12],
            running[13],
        ),
        "dp",
    )
    (
        grad_gate,
        grad_inner,
        grad_step,
        grad_shared,
        grad_kernel,
        grad_offset,
        grad_bias,
        grad_rate,
        grad_skip,
        grad_gain,
        grad_out,
    ) = reduced
    shared_sums = lax.psum((running[0], running[7], running[8]), ("dp", "tensor"))
    return (
        jnp.stack(outputs),
        jnp.stack(input_grads),
        shared_sums[0],
        grad_gate,
        grad_inner,
        grad_step,
        grad_shared,
        grad_kernel,
        grad_offset,
        shared_sums[1],
        shared_sums[2],
        grad_bias,
        grad_rate,
        grad_skip,
        grad_gain,
        grad_out,
    )


def solution(mesh):
    placed = (
        P("dp", "tensor", None),
        P(),
        P(None, "tensor"),
        P(None, "tensor"),
        P(None, "tensor"),
        P(),
        P(None, "tensor"),
        P("tensor"),
        P(),
        P(),
        P("tensor"),
        P("tensor"),
        P("tensor"),
        P("tensor"),
        P("tensor", None),
        P("dp", "tensor", None),
        P("dp", None),
        P("dp", None),
    )
    return jax.shard_map(
        body,
        mesh=mesh,
        in_specs=placed,
        out_specs=(
            P("dp", "tensor", None),
            P("dp", "tensor", None),
            P(),
            P(None, "tensor"),
            P(None, "tensor"),
            P(None, "tensor"),
            P(),
            P(None, "tensor"),
            P("tensor"),
            P(),
            P(),
            P("tensor"),
            P("tensor"),
            P("tensor"),
            P("tensor"),
            P("tensor", None),
        ),
        check_vma=False,
    )
```

profile of v0, /device:TPU:0, one launch (start us, length us, event | category | flops | bytes accessed | tf_op | source)
XLA Modules:
  0.0 1913.7 jit_solution(8220009131876546524)
XLA Ops:
  28.7 22.6 %all-gather.9.cloned.1.call-done = bf16[1024,2048]{1,0:T(8,128)(2,1)} async-done(((bf16[256,2048]{1,0:T(8,128)(2,1)}), bf16[1024,2048]{1,0:T(8,128)(2,1)}) %all-gather.9.cloned.1.call-update) | async-done | bytes 4194320 | tf_op jit(solution)/shard_map/all_gather | solution.py:172
  58.2 29.8 %all-gather.7.cloned.1.call-done = bf16[1024,2048]{1,0:T(8,128)(2,1)} async-done(((bf16[256,2048]{1,0:T(8,128)(2,1)}), bf16[1024,2048]{1,0:T(8,128)(2,1)}) %all-gather.7.cloned.1.call-update) | async-done | bytes 4194320 | tf_op jit(solution)/shard_map/all_gather | solution.py:172
  121.1 19.4 %fusion.71 = (f32[1024,1024]{1,0:T(8,128)}, f32[1024,1024]{1,0:T(8,128)}, f32[1024,1024]{1,0:T(8,128)}, f32[1024,1024]{1,0:T(8,128)}) fusion(f32[1024,1024]{1,0:T(8,128)} %fusion.234, f32[1024]{0:T(1024)S(1)} %bitcast.580, f32[1024]{0:T(1024)S(1)} %bitcast.582, f32[1024]{0:T(1024)S(1)} %bitcast.578, f32[1024]{0:T(1024)S(1)} %bitcast.576, ...), kind=kLoop, calls=%fused_computation.158 | loop fusion | flops 25165824 | bytes 25186304 | tf_op jit(solution)/shard_map/jvp()/mul | solution.py:15
  180.1 17.4 copy.550
  225.7 22.0 %fusion.67 = f32[4,256,16,64]{1,3,0,2:T(8,128)} fusion(f32[4,16,64,256]{3,2,1,0:T(8,128)S(1)} %fusion.235, f32[4,256,16]{1,0,2:T(4,128)S(1)} %copy-done.112, f32[16,4,256]{2,1,0:T(4,128)S(1)} %copy.533, f32[4,256,256]{2,1,0:T(8,128)S(1)} %fusion.233, pred[4,256,256]{2,1,0:T(8,128)(4,1)S(1)} %copy-done.99, f32[4,256,16,64]{1,3,2,0:T(8,128)S(1)} %copy-done.5, ...), kind=kOutput, calls=%fused_computation.123 | convolution fusion | flops 3245342720 | bytes 14090240 | tf_op jit(solution)/shard_map/jvp(hcts,hcsp->hctp)/dot_general | solution.py:55
  247.8 21.6 %fusion.66 = f32[4,256,16,64]{1,3,0,2:T(8,128)} fusion(f32[4,16,64,256]{3,2,1,0:T(8,128)S(1)} %fusion.239, f32[4,256,16]{1,0,2:T(4,128)S(1)} %copy-done.111, f32[16,4,256]{2,1,0:T(4,128)S(1)} %copy.546, f32[4,256,256]{2,1,0:T(8,128)S(1)} %fusion.237, pred[4,256,256]{2,1,0:T(8,128)(4,1)S(1)} %copy-done.97, f32[4,256,16,64]{1,3,2,0:T(8,128)S(1)} %copy-done.7, ...), kind=kOutput, calls=%fused_computation.121 | convolution fusion | flops 3245342720 | bytes 14090240 | tf_op jit(solution)/shard_map/jvp(hcts,hcsp->hctp)/dot_general | solution.py:55
  321.8 16.5 multiply_reduce_fusion.17
  354.4 13.7 multiply_reduce_fusion.1
  373.9 20.4 %multiply_reduce_fusion.2 = (f32[1024]{0:T(1024)}, f32[1024,1024]{1,0:T(8,128)}, bf16[1024,1024]{1,0:T(8,128)(2,1)}, bf16[1024,1024]{1,0:T(8,128)(2,1)}, f32[1024]{0:T(1024)}, /*index=5*/f32[1024,1024]{1,0:T(8,128)}) fusion(f32[1024,1024]{1,0:T(8,128)} %get-tuple-element.659, f32[1024,1024]{1,0:T(8,128)} %fusion.240, f32[1024]{0:T(1024)S(1)} %get-tuple-element.580, ...), kind=kLoop, calls=%fused_computation.126 | loop fusion | flops 54523904 | bytes 54566912 | tf_op jit(solution)/shard_map/transpose(jvp())/reduce_sum | solution.py:117
  411.3 32.3 %fusion.170 = (f32[16,4,256]{2,1,0:T(4,128)}, f32[16,4,256]{2,1,0:T(4,128)}, f32[4,256,256]{2,1,0:T(8,128)}, f32[16,4,256,256]{3,2,1,0:T(8,128)}) fusion(f32[4,256,256]{2,1,0:T(8,128)S(1)} %copy-done.82, pred[4,256,256]{2,1,0:T(8,128)(4,1)S(1)} %copy-done.99, f32[16,4,256]{2,1,0:T(4,128)S(1)} %copy.533, f32[4,256,16,64]{1,0,3,2:T(4,128)S(1)} %copy-done.3, ...), kind=kOutput, calls=%fused_computation.301 | convolution fusion | flops 3297476608 | bytes 27787264 | tf_op jit(solution)/shard_map/transpose(jvp(hcts,hcsp->hctp))/dot_general | solution.py:55
  460.6 32.7 %fusion.172 = (f32[16,4,256]{2,1,0:T(4,128)S(1)}, f32[16,4,256]{2,1,0:T(4,128)S(1)}, f32[4,256,256]{2,1,0:T(8,128)}, f32[16,4,256,256]{3,2,1,0:T(8,128)}) fusion(f32[4,256,256]{2,1,0:T(8,128)S(1)} %copy-done.80, pred[4,256,256]{2,1,0:T(8,128)(4,1)S(1)} %copy-done.98, f32[16,4,256]{2,1,0:T(4,128)S(1)} %copy-done.110, f32[4,256,16,64]{1,0,3,2:T(4,128)S(1)} %copy-done.1, ...), kind=kOutput, calls=%fused_computation.303 | convolution fusion | flops 3297476608 | bytes 27787264 | tf_op jit(solution)/shard_map/transpose(jvp(hcts,hcsp->hctp))/dot_general | solution.py:55
  518.4 11.9 while.71
  549.0 12.0 while.70
  570.2 10.8 fusion.243
  591.3 18.0 bitcast_add_fusion.5
  640.1 17.9 bitcast_add_fusion.4
  678.5 24.3 %multiply_reduce_fusion.11 = (f32[1024]{0:T(1024)}, f32[1024]{0:T(1024)}, f32[1024]{0:T(1024)}, f32[1024]{0:T(1024)}, f32[1024]{0:T(1024)}, /*index=5*/f32[1024,...) fusion(f32[1024,1024]{1,0:T(8,128)} %fusion.234, ...), kind=kLoop, calls=%fused_computation.135 | loop fusion | flops 44029952 | bytes 50376704 | tf_op jit(solution)/shard_map/transpose(jvp())/reduce_sum | solution.py:24
  762.6 11.8 fusion.208
  775.0 11.5 fusion.209
  833.7 76.4 %all-reduce.54 = (bf16[1024,256]{1,0:T(8,128)(2,1)}, bf16[1024,256]{1,0:T(8,128)(2,1)}) all-reduce(f32[1024,256]{1,0:T(8,128)S(1)} %pad_add_fusion.6, f32[1024,256]{1,0:T(8,128)S(1)} %pad_add_fusion.9), channel_id=1, replica_groups=mesh['dp'=8,'tensor'=4] {'tensor'}, use_global_device_ids=true, to_apply=%region_48.50 | all-reduce | flops 524288 | bytes 3145728 | tf_op jit(solution)/shard_map/psum | solution.py:220
  964.2 37.8 %all-reduce.45 = (f32[4,1024]{1,0:T(4,128)}, f32[1024]{0:T(1024)}, f32[16]{0:T(128)}, f32[16]{0:T(128)}, f32[16]{0:T(128)}, /*index=5*/f32[1024]{0:T(1024)}) all-reduce(f32[4,1024]{1,0:T(4,128)S(1)} %add_add_fusion.2, f32[1024]{0:T(1024)S(1)} %add.459, f32[16]{0:T(128)S(1)} %add.462, ...), channel_id=1, replica_groups=mesh['dp'=8,'tensor'=4] {'dp'}, use_global_device_ids=true, to_apply=%region_65.67 | all-reduce | flops 6192 | bytes 49536 | tf_op jit(solution)/shard_map/psum | solution.py:262
  1011.6 37.5 %all-reduce.44 = (f32[2048]{0:T(1024)}, f32[4,256]{1,0:T(4,128)}, f32[256]{0:T(256)}) all-reduce(f32[2048]{0:T(1024)S(1)} %add.453, f32[4,256]{1,0:T(4,128)S(1)} %add_add_fusion.3, f32[256]{0:T(256)S(1)} %add.461), channel_id=1, replica_groups=mesh['dp'=8,'tensor'=4] {'dp','tensor'}, use_global_device_ids=true, to_apply=%region_52.54 | all-reduce | flops 3328 | bytes 26624 | tf_op jit(solution)/shard_map/psum | solution.py:291
  1049.1 20.9 %reduce-scatter.7.cloned.1.call-done = f32[256,2048]{1,0:T(8,128)} async-done(((f32[1024,2048]{1,0:T(8,128)}), f32[256,2048]{1,0:T(8,128)}) %reduce-scatter.7.cloned.1.call-update) | async-done | bytes 2097168 | tf_op jit(solution)/shard_map/reduce_scatter | solution.py:195
  1078.0 810.2 %all-reduce.53.cloned.1.call-done = (f32[2048,1024]{1,0:T(8,128)}, f32[2048,1024]{1,0:T(8,128)}, f32[2048,16]{0,1:T(8,128)}, f32[2048,256]{1,0:T(8,128)}, f32[1024,2048]{1,0:T(8,128)}) async-done(((f32[2048,1024]{1,0:T(8,128)}, f32[2048,1024]{1,0:T(8,128)}, f32[2048,16]{0,1:T(8,128)}, f32[2048,256]{1,0:T(8,128)}, f32[1024,2048]{1,0:T(8,128)}), (f32[2048,1024]{1,0:T(8,128)}, f32[2048,1024]{1,0:T(8,128)}, ...) | async-done | bytes 27394064 | tf_op jit(solution)/shard_map/psum | solution.py:262
  (673 shorter events, 584.3 us)
Async XLA Ops:
  7.2 91.8 %copy-start = (bf16[2048,256]{1,0:T(8,128)(2,1)S(1)}, bf16[2048,256]{1,0:T(8,128)(2,1)}, u32[]{:S(2)}) copy-start(bf16[2048,256]{1,0:T(8,128)(2,1)} %param.32) | copy-start | bytes 3145732
  7.2 44.2 %all-gather.9.cloned.1.call-start = ((), (), s32[]{:S(2)}) async-start(), calls=%async_computation.6 | async-start | bytes 5242880 | tf_op jit(solution)/shard_map/all_gather | solution.py:172
  14.1 74.0 %all-gather.7.cloned.1.call-start = ((), (), s32[]{:S(2)}) async-start(), calls=%async_computation.4 | async-start | bytes 5242880 | tf_op jit(solution)/shard_map/all_gather | solution.py:172
  14.8 329.6 %all-gather.13.cloned.1.call-start = ((), (), s32[]{:S(2)}) async-start(), calls=%async_computation.11 | async-start | bytes 5242880 | tf_op jit(solution)/shard_map/all_gather | solution.py:203
  16.4 338.0 %all-gather.11.cloned.1.call-start = ((), (), s32[]{:S(2)}) async-start(), calls=%async_computation.10 | async-start | bytes 5242880 | tf_op jit(solution)/shard_map/all_gather | solution.py:203
  17.0 985.1 %reduce-scatter.11.cloned.1.call-start = ((), (), s32[]{:S(2)}) async-start(), calls=%async_computation.9 | async-start | bytes 10485760 | tf_op jit(solution)/shard_map/reduce_scatter | solution.py:243
  19.4 84.4 %copy-start.152 = (f32[1,256]{1,0:T(1,128)}, f32[1,256]{1,0:T(1,128)S(1)}, u32[]{:S(2)}) copy-start(f32[1,256]{1,0:T(1,128)S(1)} %get-tuple-element.699) | copy-start | bytes 3076
  19.4 84.4 %copy-start.154 = (f32[1,256]{1,0:T(1,128)}, f32[1,256]{1,0:T(1,128)S(1)}, u32[]{:S(2)}) copy-start(f32[1,256]{1,0:T(1,128)S(1)} %get-tuple-element.700) | copy-start | bytes 3076
  19.5 84.4 %copy-start.156 = (f32[1,256]{1,0:T(1,128)}, f32[1,256]{1,0:T(1,128)S(1)}, u32[]{:S(2)}) copy-start(f32[1,256]{1,0:T(1,128)S(1)} %get-tuple-element.701) | copy-start | bytes 3076
  19.5 84.4 %copy-start.158 = (f32[1,256]{1,0:T(1,128)}, f32[1,256]{1,0:T(1,128)S(1)}, u32[]{:S(2)}) copy-start(f32[1,256]{1,0:T(1,128)S(1)} %get-tuple-element.702) | copy-start | bytes 3076
  19.6 354.2 %copy-start.119 = (f32[1024]{0:T(1024)}, f32[1024]{0:T(1024)S(1)}, u32[]{:S(2)}) copy-start(f32[1024]{0:T(1024)S(1)} %mul.1247) | copy-start | bytes 12292
  20.2 100.9 %copy-start.121 = (f32[1,1024]{1,0:T(1,128)}, f32[1,1024]{1,0:T(1,128)S(1)}, u32[]{:S(2)}) copy-start(f32[1,1024]{1,0:T(1,128)S(1)} %get-tuple-element.664) | copy-start | bytes 12292
  20.2 100.9 %copy-start.123 = (f32[1,1024]{1,0:T(1,128)}, f32[1,1024]{1,0:T(1,128)S(1)}, u32[]{:S(2)}) copy-start(f32[1,1024]{1,0:T(1,128)S(1)} %get-tuple-element.665) | copy-start | bytes 12292
  20.2 100.9 %copy-start.125 = (f32[1,1024]{1,0:T(1,128)}, f32[1,1024]{1,0:T(1,128)S(1)}, u32[]{:S(2)}) copy-start(f32[1,1024]{1,0:T(1,128)S(1)} %get-tuple-element.666) | copy-start | bytes 12292
  58.2 189.5 %copy-start.109 = (f32[16,4,256]{2,1,0:T(4,128)}, f32[16,4,256]{2,1,0:T(4,128)S(1)}, u32[]{:S(2)}) copy-start(f32[16,4,256]{2,1,0:T(4,128)S(1)} %copy.546) | copy-start | bytes 196612
  94.9 152.8 %copy-start.70 = (f32[2,4,8,256]{3,2,0,1:T(8,128)}, f32[2,4,8,256]{3,2,0,1:T(8,128)S(1)}, u32[]{:S(2)}) copy-start(f32[2,4,8,256]{3,2,0,1:T(8,128)S(1)} %copy.764) | copy-start | bytes 196612
  96.3 101.3 %copy-start.75 = (f32[16,4,256]{2,0,1:T(8,128)}, f32[16,4,256]{2,0,1:T(8,128)S(1)}, u32[]{:S(2)}) copy-start(f32[16,4,256]{2,0,1:T(8,128)S(1)} %get-tuple-element.651) | copy-start | bytes 196612
  96.9 464.2 %copy-start.73 = (f32[2,4,8,256]{3,2,0,1:T(8,128)}, f32[2,4,8,256]{3,2,0,1:T(8,128)S(1)}, u32[]{:S(2)}) copy-start(f32[2,4,8,256]{3,2,0,1:T(8,128)S(1)} %copy.765) | copy-start | bytes 196612
  107.4 107.4 %copy-start.36 = (f32[1024,128]{1,0:T(8,128)}, f32[1024,128]{1,0:T(8,128)S(1)}, u32[]{:S(2)}) copy-start(f32[1024,128]{1,0:T(8,128)S(1)} %get-tuple-element.641) | copy-start | bytes 1572868
  109.1 108.0 %copy-start.33 = (f32[1024,128]{1,0:T(8,128)}, f32[1024,128]{1,0:T(8,128)S(1)}, u32[]{:S(2)}) copy-start(f32[1024,128]{1,0:T(8,128)S(1)} %get-tuple-element.643) | copy-start | bytes 1572868
  739.0 267.1 %reduce-scatter.9.cloned.1.call-start = ((), (), s32[]{:S(2)}) async-start(), calls=%async_computation.8 | async-start | bytes 10485760 | tf_op jit(solution)/shard_map/reduce_scatter | solution.py:243
  761.9 287.2 %reduce-scatter.5.cloned.1.call-start = ((), (), s32[]{:S(2)}) async-start(), calls=%async_computation.5 | async-start | bytes 10485760 | tf_op jit(solution)/shard_map/reduce_scatter | solution.py:195
  774.4 295.6 %reduce-scatter.7.cloned.1.call-start = ((), (), s32[]{:S(2)}) async-start(), calls=%async_computation.7 | async-start | bytes 10485760 | tf_op jit(solution)/shard_map/reduce_scatter | solution.py:195
  786.6 1101.6 %all-reduce.53.cloned.1.call-start = ((), (), s32[]{:S(2)}) async-start(), calls=%async_computation.12 | async-start | bytes 54788096 | tf_op jit(solution)/shard_map/psum | solution.py:262
  (180 other events, 2383.9 us)
Sparse Core Ops, SparseCore 0:
  14.2 37.1 all-gather.8
  53.5 34.4 all-gather.6
  89.6 34.5 all-gather.12
  125.6 34.5 all-gather.10
  739.1 72.4 reduce-scatter.10
  814.8 104.1 reduce-scatter.8
  921.5 72.5 reduce-scatter.4
  997.5 72.4 reduce-scatter.6
  1075.8 812.2 all-reduce.52
where the time goes:
time: 1930 us; the launch traced here: 1910 us
  waiting for transfers between devices  885 us (46%)
  matrix products  439 us (23%)
  local copies, waits for them, and re-layouts  213 us (11%)
  other arithmetic  193 us (10%)
  blocking collectives  164 us (8%)
  between operations  19.4 us (1%)
    psum x1, waiting for transfers between devices, body(): lax.psum((running[1], running[2], running[3], running[4], running[5], run...  810 us
    dot_general x6, matrix products, state_scan(): jnp.einsum('hcts,hcsp->hctp', mixing, weighted_x, precision=HIGHEST)  145 us
    psum x1, blocking collectives, body(): shared_full = lax.psum(pieces_grad[3], 'tensor')  76.4 us
    all_gather x2, waiting for transfers between devices, body(): normed_in = lax.all_gather(normed_rows, 'tensor', axis=0, tiled=True)  52.4 us
    dot_general x6, matrix products, state_scan(): jnp.einsum('hcsp,csn->chpn', to_end[:, :, :, None] * weighted_x, b_blocks...  49.4 us
    reshape x6, local copies, waits for them, and re-layouts, state_scan(): return total.reshape(length, head_count, head_width)  43 us
    another operation x14, other arithmetic  41.7 us
    reshape x6, local copies, waits for them, and re-layouts, state_scan(): (inputs_x * step_size[:, :, None]).reshape(pieces, block_len, head_count,...  41 us
  transfers between devices with their start and end apart: 9, of which 4 were waited for; matrix products, arithmetic and copies ran while one was open for 23% of the time, Pallas kernels for 0%

commit v1 on v0

--- a/solution.py
+++ b/solution.py
@@ -217,7 +217,7 @@
         pieces_grad = mixer_pullback(gated_grad)
         for slot_index in range(4, 11):
             running[slot_index + 1] = running[slot_index + 1] + pieces_grad[slot_index]
-        shared_full = lax.psum(pieces_grad[3], "tensor")
+        shared_full = jnp.sum(lax.all_gather(pieces_grad[3], "tensor"), axis=0)
         gate_low = pieces_grad[0].astype(jnp.bfloat16)
         inner_low = pieces_grad[1].astype(jnp.bfloat16)
         step_low = pieces_grad[2].astype(jnp.bfloat16)

time: 1930 us -> 1940 us (level)
  waiting for transfers between devices: 885 us -> 965 us
  blocking collectives: 164 us -> 87.3 us
    reduce_scatter x2, waiting for transfers between devices: 20.9 us -> 101 us  [body(): lax.psum_scatter(jnp.dot(normed_out, weight_out, preferred_element_type=j...]
    psum x1 -> x0, blocking collectives: 76.4 us -> none  [body(): shared_full = lax.psum(pieces_grad[3], 'tensor')]
  transfers between devices with their start and end apart: 9 -> 11, of which waited for: 4 -> 5; matrix products, arithmetic and copies ran while one was open for 23% -> 32% of each run, Pallas kernels for 0% -> 0%
where the time goes in v1:
time: 1940 us; the launch traced here: 1930 us
  waiting for transfers between devices  965 us (50%)
  matrix products  434 us (22%)
  local copies, waits for them, and re-layouts  211 us (11%)
  other arithmetic  210 us (11%)
  blocking collectives  87.3 us (4%)
  between operations  19.5 us (1%)
    psum x1, waiting for transfers between devices, body(): lax.psum((running[1], running[2], running[3], running[4], running[5], run...  810 us
    dot_general x6, matrix products, state_scan(): jnp.einsum('hcts,hcsp->hctp', mixing, weighted_x, precision=HIGHEST)  146 us
    reduce_scatter x2, waiting for transfers between devices, body(): lax.psum_scatter(jnp.dot(normed_out, weight_out, preferred_element_type=j...  101 us
    all_gather x2, waiting for transfers between devices, body(): normed_in = lax.all_gather(normed_rows, 'tensor', axis=0, tiled=True)  52.5 us
    dot_general x6, matrix products, state_scan(): jnp.einsum('hcsp,csn->chpn', to_end[:, :, :, None] * weighted_x, b_blocks...  46.7 us
    reshape x6, local copies, waits for them, and re-layouts, state_scan(): return total.reshape(length, head_count, head_width)  43.4 us
    another operation x14, other arithmetic  42.9 us
    reshape x4, local copies, waits for them, and re-layouts, state_mixer(): inputs_x = activated.reshape(length, head_count, -1)  39.7 us
  transfers between devices with their start and end apart: 11, of which 5 were waited for; matrix products, arithmetic and copies ran while one was open for 32% of the time, Pallas kernels for 0%

profile of v1, /device:TPU:0, one launch (start us, length us, event | category | flops | bytes accessed | tf_op | source)
XLA Modules:
  0.0 1928.3 jit_solution(8218082993572906661)
XLA Ops:
  28.7 22.7 %all-gather.13.cloned.1.call-done = bf16[1024,2048]{1,0:T(8,128)(2,1)} async-done(((bf16[256,2048]{1,0:T(8,128)(2,1)}), bf16[1024,2048]{1,0:T(8,128)(2,1)}) %all-gather.13.cloned.1.call-update) | async-done | bytes 4194320 | tf_op jit(solution)/shard_map/all_gather | solution.py:172
  58.3 29.8 %all-gather.11.cloned.1.call-done = bf16[1024,2048]{1,0:T(8,128)(2,1)} async-done(((bf16[256,2048]{1,0:T(8,128)(2,1)}), bf16[1024,2048]{1,0:T(8,128)(2,1)}) %all-gather.11.cloned.1.call-update) | async-done | bytes 4194320 | tf_op jit(solution)/shard_map/all_gather | solution.py:172
  121.1 19.5 %fusion.71 = (f32[1024,1024]{1,0:T(8,128)}, f32[1024,1024]{1,0:T(8,128)}, f32[1024,1024]{1,0:T(8,128)}, f32[1024,1024]{1,0:T(8,128)}) fusion(f32[1024,1024]{1,0:T(8,128)} %fusion.234, f32[1024]{0:T(1024)S(1)} %bitcast.582, f32[1024]{0:T(1024)S(1)} %bitcast.584, f32[1024]{0:T(1024)S(1)} %bitcast.580, f32[1024]{0:T(1024)S(1)} %bitcast.578, ...), kind=kLoop, calls=%fused_computation.158 | loop fusion | flops 25165824 | bytes 25186304 | tf_op jit(solution)/shard_map/jvp()/mul | solution.py:15
  180.1 17.5 copy.550
  227.5 22.1 %fusion.67 = f32[4,256,16,64]{1,3,0,2:T(8,128)} fusion(f32[4,16,64,256]{3,2,1,0:T(8,128)S(1)} %fusion.235, f32[4,256,16]{1,0,2:T(4,128)S(1)} %copy-done.111, f32[16,4,256]{2,1,0:T(4,128)S(1)} %copy.533, f32[4,256,256]{2,1,0:T(8,128)S(1)} %fusion.233, pred[4,256,256]{2,1,0:T(8,128)(4,1)S(1)} %copy-done.95, f32[4,256,16,64]{1,3,2,0:T(8,128)S(1)} %copy-done.5, ...), kind=kOutput, calls=%fused_computation.123 | convolution fusion | flops 3245342720 | bytes 14090240 | tf_op jit(solution)/shard_map/jvp(hcts,hcsp->hctp)/dot_general | solution.py:55
  249.7 21.6 %fusion.66 = f32[4,256,16,64]{1,3,0,2:T(8,128)} fusion(f32[4,16,64,256]{3,2,1,0:T(8,128)S(1)} %fusion.239, f32[4,256,16]{1,0,2:T(4,128)S(1)} %copy-done.110, f32[16,4,256]{2,1,0:T(4,128)S(1)} %copy.546, f32[4,256,256]{2,1,0:T(8,128)S(1)} %fusion.237, pred[4,256,256]{2,1,0:T(8,128)(4,1)S(1)} %copy-done.93, f32[4,256,16,64]{1,3,2,0:T(8,128)S(1)} %copy-done.7, ...), kind=kOutput, calls=%fused_computation.121 | convolution fusion | flops 3245342720 | bytes 14090240 | tf_op jit(solution)/shard_map/jvp(hcts,hcsp->hctp)/dot_general | solution.py:55
  313.0 17.6 multiply_reduce_fusion.17
  346.7 13.7 multiply_reduce_fusion.1
  366.3 20.2 %multiply_reduce_fusion.2 = (f32[1024]{0:T(1024)}, f32[1024,1024]{1,0:T(8,128)}, bf16[1024,1024]{1,0:T(8,128)(2,1)}, bf16[1024,1024]{1,0:T(8,128)(2,1)}, f32[1024]{0:T(1024)}, /*index=5*/f32[1024,1024]{1,0:T(8,128)}) fusion(f32[1024,1024]{1,0:T(8,128)} %get-tuple-element.657, f32[1024,1024]{1,0:T(8,128)} %fusion.240, f32[1024]{0:T(1024)S(1)} %get-tuple-element.578, ...), kind=kLoop, calls=%fused_computation.126 | loop fusion | flops 54523904 | bytes 54566912 | tf_op jit(solution)/shard_map/transpose(jvp())/reduce_sum | solution.py:117
  440.7 33.5 %fusion.170 = (f32[16,4,256]{2,1,0:T(4,128)}, f32[16,4,256]{2,1,0:T(4,128)}, f32[4,256,256]{2,1,0:T(8,128)S(1)}, f32[16,4,256,256]{3,2,1,0:T(8,128)}) fusion(f32[4,256,256]{2,1,0:T(8,128)S(1)} %copy-done.78, pred[4,256,256]{2,1,0:T(8,128)(4,1)S(1)} %copy-done.96, f32[16,4,256]{2,1,0:T(4,128)S(1)} %copy.533, f32[4,256,16,64]{1,0,3,2:T(4,128)S(1)} %copy-done.4, ...), kind=kOutput, calls=%fused_computation.301 | convolution fusion | flops 3297476608 | bytes 27787264 | tf_op jit(solution)/shard_map/transpose(jvp(hcts,hcsp->hctp))/dot_general | solution.py:55
  474.2 33.6 %fusion.172 = (f32[16,4,256]{2,1,0:T(4,128)}, f32[16,4,256]{2,1,0:T(4,128)}, f32[4,256,256]{2,1,0:T(8,128)}, f32[16,4,256,256]{3,2,1,0:T(8,128)}) fusion(f32[4,256,256]{2,1,0:T(8,128)S(1)} %copy-done.76, pred[4,256,256]{2,1,0:T(8,128)(4,1)S(1)} %copy-done.94, f32[16,4,256]{2,1,0:T(4,128)S(1)} %copy-done.109, f32[4,256,16,64]{1,0,3,2:T(4,128)S(1)} %copy-done.2, ...), kind=kOutput, calls=%fused_computation.303 | convolution fusion | flops 3297476608 | bytes 27787264 | tf_op jit(solution)/shard_map/transpose(jvp(hcts,hcsp->hctp))/dot_general | solution.py:55
  509.4 11.8 while.71
  532.3 12.2 while.70
  617.9 17.9 bitcast_add_fusion.5
  657.5 16.8 bitcast_add_fusion.4
  698.0 28.3 %multiply_reduce_fusion.11 = (f32[1024]{0:T(1024)}, f32[1024]{0:T(1024)}, f32[1024]{0:T(1024)}, f32[1024]{0:T(1024)}, f32[1024]{0:T(1024)}, /*index=5*/f32[1024,...) fusion(f32[1024,1024]{1,0:T(8,128)} %fusion.234, ...), kind=kLoop, calls=%fused_computation.135 | loop fusion | flops 44029952 | bytes 50376704 | tf_op jit(solution)/shard_map/transpose(jvp())/reduce_sum | solution.py:24
  746.6 11.6 broadcast_multiply_fusion
  810.1 11.9 fusion.208
  822.7 11.5 fusion.209
  899.5 37.9 %all-reduce.45 = (f32[4,1024]{1,0:T(4,128)}, f32[1024]{0:T(1024)}, f32[16]{0:T(128)}, f32[16]{0:T(128)}, f32[16]{0:T(128)}, /*index=5*/f32[1024]{0:T(1024)}) all-reduce(f32[4,1024]{1,0:T(4,128)S(1)} %add_add_fusion.2, f32[1024]{0:T(1024)S(1)} %add.455, f32[16]{0:T(128)S(1)} %add.458, ...), channel_id=1, replica_groups=mesh['dp'=8,'tensor'=4] {'dp'}, use_global_device_ids=true, to_apply=%region_65.67 | all-reduce | flops 6192 | bytes 49536 | tf_op jit(solution)/shard_map/psum | solution.py:262
  946.2 37.5 %all-reduce.44 = (f32[2048]{0:T(1024)}, f32[4,256]{1,0:T(4,128)}, f32[256]{0:T(256)}) all-reduce(f32[2048]{0:T(1024)S(1)} %add.449, f32[4,256]{1,0:T(4,128)S(1)} %add_add_fusion.3, f32[256]{0:T(256)S(1)} %add.457), channel_id=1, replica_groups=mesh['dp'=8,'tensor'=4] {'dp','tensor'}, use_global_device_ids=true, to_apply=%region_52.54 | all-reduce | flops 3328 | bytes 26624 | tf_op jit(solution)/shard_map/psum | solution.py:291
  983.7 25.9 %reduce-scatter.5.cloned.1.call-done = f32[256,2048]{1,0:T(8,128)} async-done(((f32[1024,2048]{1,0:T(8,128)}), f32[256,2048]{1,0:T(8,128)}) %reduce-scatter.5.cloned.1.call-update) | async-done | bytes 2097168 | tf_op jit(solution)/shard_map/reduce_scatter | solution.py:195
  1009.6 74.9 %reduce-scatter.7.cloned.1.call-done = f32[256,2048]{1,0:T(8,128)} async-done(((f32[1024,2048]{1,0:T(8,128)}), f32[256,2048]{1,0:T(8,128)}) %reduce-scatter.7.cloned.1.call-update) | async-done | bytes 2097168 | tf_op jit(solution)/shard_map/reduce_scatter | solution.py:195
  1092.5 810.4 %all-reduce.51.cloned.1.call-done = (f32[2048,1024]{1,0:T(8,128)}, f32[2048,1024]{1,0:T(8,128)}, f32[2048,16]{0,1:T(8,128)}, f32[2048,256]{1,0:T(8,128)}, f32[1024,2048]{1,0:T(8,128)}) async-done(((f32[2048,1024]{1,0:T(8,128)}, f32[2048,1024]{1,0:T(8,128)}, f32[2048,16]{0,1:T(8,128)}, f32[2048,256]{1,0:T(8,128)}, f32[1024,2048]{1,0:T(8,128)}), (f32[2048,1024]{1,0:T(8,128)}, f32[2048,1024]{1,0:T(8,128)}, ...) | async-done | bytes 27394064 | tf_op jit(solution)/shard_map/psum | solution.py:262
  (698 shorter events, 588.0 us)
Async XLA Ops:
  7.2 91.9 %copy-start = (bf16[2048,256]{1,0:T(8,128)(2,1)S(1)}, bf16[2048,256]{1,0:T(8,128)(2,1)}, u32[]{:S(2)}) copy-start(bf16[2048,256]{1,0:T(8,128)(2,1)} %param.32) | copy-start | bytes 3145732
  7.2 44.2 %all-gather.13.cloned.1.call-start = ((), (), s32[]{:S(2)}) async-start(), calls=%async_computation.6 | async-start | bytes 5242880 | tf_op jit(solution)/shard_map/all_gather | solution.py:172
  14.1 74.0 %all-gather.11.cloned.1.call-start = ((), (), s32[]{:S(2)}) async-start(), calls=%async_computation.4 | async-start | bytes 5242880 | tf_op jit(solution)/shard_map/all_gather | solution.py:172
  14.9 321.9 %all-gather.19.cloned.1.call-start = ((), (), s32[]{:S(2)}) async-start(), calls=%async_computation.12 | async-start | bytes 5242880 | tf_op jit(solution)/shard_map/all_gather | solution.py:203
  16.4 330.4 %all-gather.15.cloned.1.call-start = ((), (), s32[]{:S(2)}) async-start(), calls=%async_computation.10 | async-start | bytes 5242880 | tf_op jit(solution)/shard_map/all_gather | solution.py:203
  17.0 869.2 %all-gather.21.cloned.1.call-start = ((), (), s32[]{:S(2)}) async-start(), calls=%async_computation.13 | async-start | bytes 5242880 | tf_op jit(solution)/shard_map/all_gather | solution.py:220
  19.4 84.5 %copy-start.153 = (f32[1,256]{1,0:T(1,128)}, f32[1,256]{1,0:T(1,128)S(1)}, u32[]{:S(2)}) copy-start(f32[1,256]{1,0:T(1,128)S(1)} %get-tuple-element.697) | copy-start | bytes 3076
  19.4 84.5 %copy-start.155 = (f32[1,256]{1,0:T(1,128)}, f32[1,256]{1,0:T(1,128)S(1)}, u32[]{:S(2)}) copy-start(f32[1,256]{1,0:T(1,128)S(1)} %get-tuple-element.698) | copy-start | bytes 3076
  19.6 346.6 %copy-start.120 = (f32[1024]{0:T(1024)}, f32[1024]{0:T(1024)S(1)}, u32[]{:S(2)}) copy-start(f32[1024]{0:T(1024)S(1)} %mul.1247) | copy-start | bytes 12292
  20.2 100.9 %copy-start.122 = (f32[1,1024]{1,0:T(1,128)}, f32[1,1024]{1,0:T(1,128)S(1)}, u32[]{:S(2)}) copy-start(f32[1,1024]{1,0:T(1,128)S(1)} %get-tuple-element.662) | copy-start | bytes 12292
  20.2 100.9 %copy-start.124 = (f32[1,1024]{1,0:T(1,128)}, f32[1,1024]{1,0:T(1,128)S(1)}, u32[]{:S(2)}) copy-start(f32[1,1024]{1,0:T(1,128)S(1)} %get-tuple-element.663) | copy-start | bytes 12292
  20.2 100.9 %copy-start.126 = (f32[1,1024]{1,0:T(1,128)}, f32[1,1024]{1,0:T(1,128)S(1)}, u32[]{:S(2)}) copy-start(f32[1,1024]{1,0:T(1,128)S(1)} %get-tuple-element.664) | copy-start | bytes 12292
  58.3 191.4 %copy-start.108 = (f32[16,4,256]{2,1,0:T(4,128)}, f32[16,4,256]{2,1,0:T(4,128)S(1)}, u32[]{:S(2)}) copy-start(f32[16,4,256]{2,1,0:T(4,128)S(1)} %copy.546) | copy-start | bytes 196612
  94.9 154.7 %copy-start.69 = (f32[2,4,8,256]{3,2,0,1:T(8,128)}, f32[2,4,8,256]{3,2,0,1:T(8,128)S(1)}, u32[]{:S(2)}) copy-start(f32[2,4,8,256]{3,2,0,1:T(8,128)S(1)} %copy.764) | copy-start | bytes 196612
  96.3 101.3 %copy-start.71 = (f32[16,4,256]{2,0,1:T(8,128)}, f32[16,4,256]{2,0,1:T(8,128)S(1)}, u32[]{:S(2)}) copy-start(f32[16,4,256]{2,0,1:T(8,128)S(1)} %get-tuple-element.649) | copy-start | bytes 196612
  109.1 88.5 %copy-start.30 = (f32[1024,128]{1,0:T(8,128)}, f32[1024,128]{1,0:T(8,128)S(1)}, u32[]{:S(2)}) copy-start(f32[1024,128]{1,0:T(8,128)S(1)} %get-tuple-element.641) | copy-start | bytes 1572868
  566.6 322.3 %all-gather.17.cloned.1.call-start = ((), (), s32[]{:S(2)}) async-start(), calls=%async_computation.11 | async-start | bytes 5242880 | tf_op jit(solution)/shard_map/all_gather | solution.py:220
  697.9 239.6 %reduce-scatter.11.cloned.1.call-start = ((), (), s32[]{:S(2)}) async-start(), calls=%async_computation.9 | async-start | bytes 10485760 | tf_op jit(solution)/shard_map/reduce_scatter | solution.py:243
  787.1 153.9 %reduce-scatter.9.cloned.1.call-start = ((), (), s32[]{:S(2)}) async-start(), calls=%async_computation.8 | async-start | bytes 10485760 | tf_op jit(solution)/shard_map/reduce_scatter | solution.py:243
  809.4 200.2 %reduce-scatter.5.cloned.1.call-start = ((), (), s32[]{:S(2)}) async-start(), calls=%async_computation.5 | async-start | bytes 10485760 | tf_op jit(solution)/shard_map/reduce_scatter | solution.py:195
  822.0 262.5 %reduce-scatter.7.cloned.1.call-start = ((), (), s32[]{:S(2)}) async-start(), calls=%async_computation.7 | async-start | bytes 10485760 | tf_op jit(solution)/shard_map/reduce_scatter | solution.py:195
  834.2 1068.6 %all-reduce.51.cloned.1.call-start = ((), (), s32[]{:S(2)}) async-start(), calls=%async_computation.14 | async-start | bytes 54788096 | tf_op jit(solution)/shard_map/psum | solution.py:262
  940.9 143.6 %copy-start.172 = (f32[256]{0:T(256)S(1)}, f32[256]{0:T(256)}, u32[]{:S(2)}) copy-start(f32[256]{0:T(256)} %get-tuple-element.701) | copy-start | bytes 3076
  941.0 143.6 %copy-start.173 = (f32[256]{0:T(256)S(1)}, f32[256]{0:T(256)}, u32[]{:S(2)}) copy-start(f32[256]{0:T(256)} %get-tuple-element.722) | copy-start | bytes 3076
  (192 other events, 2868.0 us)
Sparse Core Ops, SparseCore 0:
  14.2 37.1 all-gather.12
  53.6 34.4 all-gather.10
  89.6 34.5 all-gather.18
  125.6 34.5 all-gather.14
  566.7 35.1 all-gather.20
  698.0 35.1 all-gather.16
  787.2 72.1 reduce-scatter.10
  862.7 71.7 reduce-scatter.8
  937.1 72.4 reduce-scatter.4
  1012.8 71.7 reduce-scatter.6
  1090.4 812.3 all-reduce.50
